TPU v7x, 512 devices: a whole 4x8x8 slice. The times are simulated.
512 devices in a mesh: pair: 64 (over z, x, core), cuts: 8 (over y).
Axes of the slice: x: 4, y: 8, z: 8, core: 2. Of those that a mesh axis runs over, the one named last changes fastest.
Arguments:
- amplitudes: bfloat16 [65536, 2048], P('pair'), may hold values from -6 to 6
- factors: bfloat16 [128, 24, 128, 128], P('pair', 'cuts'), may hold values from -0.5 to 0.5
- screening: int32 [32, 16], replicated, may hold values from 0 to 127, as said below
- tile_slot: int32 [128], replicated, may hold values from 0 to 127, as said below
- pair_orbitals: int32 [32, 2], replicated, may hold values from 0 to 3999
- occupied_energy: float32 [4000], replicated, may hold values from -2 to -0.3
- virtual_energy: float32 [128, 128], replicated, may hold values from 0.2 to 3
Outputs:
- scaled_residual: float32 [65536, 2048], P(('pair', 'cuts'))
Inputs may be any that keep to these rules, and one draw needn't show every extreme that they name: `screening`: call tile_slot[t] // 2 the owner of tile t. The 16 tiles named by one pair have 16 different owners. `tile_slot`: every tile has its own slot.
All inputs are finite; a program needn't handle non-finite values.
Results may differ from a plain program's by a relative error of at most 0.012.
Values may be sent and summed in bfloat16 or wider, within the bound.
A program may use at most 64 MiB of HBM per device.

v0:
```python
import jax
import jax.numpy as jnp
from jax import lax
from jax.sharding import PartitionSpec as P

TILE = 128
K = 16
NQ_CUT = 3


def local(
    amplitudes, factors, screening, tile_slot, pair_orbitals, occupied_energy, virtual_energy
):
    pair_index = lax.axis_index("pair")
    row_tiles = amplitudes.shape[0] // TILE
    first_tile = pair_index * row_tiles
    pair_id = first_tile // K
    tile_start = first_tile % K
    my_tiles = lax.dynamic_slice_in_dim(screening, pair_id, 1, 0).reshape(K)
    my_slots = tile_slot[my_tiles]
    segment = lax.all_gather(factors, "pair", axis=0, tiled=True)
    count = segment.shape[0]
    inside = (my_slots >= 0) & (my_slots < count)
    safe_rows = jnp.clip(my_slots, 0, count - 1)
    picked = jnp.where(inside[:, None, None, None], segment[safe_rows], jnp.zeros((), jnp.bfloat16))
    left_tiles = lax.dynamic_slice_in_dim(picked, tile_start, row_tiles, 0)
    blocks = amplitudes.reshape(row_tiles, TILE, K * TILE)
    running = jnp.zeros((row_tiles, TILE, K, TILE), jnp.float32)
    for vector in range(NQ_CUT):
        factor_left = left_tiles[:, vector]
        half_done = jnp.einsum(
            "iac,icx->iax", factor_left, blocks, preferred_element_type=jnp.float32
        )
        half_done = half_done.astype(jnp.bfloat16).reshape(row_tiles, TILE, K, TILE)
        running = running + jnp.einsum(
            "iajd,jbd->iajb", half_done, picked[:, vector], preferred_element_type=jnp.float32
        )
    partial_value = running.reshape(row_tiles * TILE, K * TILE)
    summed = lax.psum_scatter(
        partial_value.astype(jnp.bfloat16), "cuts", scatter_dimension=0, tiled=True
    ).astype(jnp.float32)
    orbitals = lax.dynamic_slice_in_dim(pair_orbitals, pair_id, 1, 0).reshape(2)
    pair_energy = occupied_energy[orbitals]
    tile_energy = virtual_energy[my_tiles].reshape(K * TILE)
    row_energy = tile_energy - pair_energy[0]
    col_energy = tile_energy - pair_energy[1]
    row_count = summed.shape[0]
    row_begin = tile_start * TILE + lax.axis_index("cuts") * row_count
    row_part = lax.dynamic_slice_in_dim(row_energy, row_begin, row_count, 0)
    return summed / (row_part[:, None] + col_energy[None, :])


def solution(mesh):
    return jax.shard_map(
        local,
        mesh=mesh,
        in_specs=(P("pair", None), P("pair", "cuts", None, None), P(), P(), P(), P(), P()),
        out_specs=P(("pair", "cuts"), None),
        check_vma=False,
    )
```

profile of v0, /device:TPU:1, one launch (start us, length us, event | category | flops | bytes accessed | tf_op | source)
XLA Modules:
  0.0 212.6 jit_solution(11448872017577413834)
XLA Ops:
  6.5 0.0 copy-start
  6.5 0.0 all-gather.2.cloned.1.call-start
  6.5 0.7 all-gather.2.cloned.1.call-update
  7.3 0.0 reduce-scatter.2.cloned.1.call-start
  7.3 0.9 dynamic-slice_reduce_fusion
  8.2 1.3 gather_fusion
  9.6 103.0 %all-gather.2.cloned.1.call-done = bf16[128,3,128,128]{3,2,1,0:T(8,128)(2,1)} async-done(((bf16[2,3,128,128]{3,2,1,0:T(8,128)(2,1)}), bf16[128,3,128,128]{3,2,1,0:T(8,128)(2,1)}) %all-gather.2.cloned.1.call-update) | async-done | bytes 12582928 | tf_op jit(solution)/shard_map/all_gather | solution.py:21
  112.6 5.4 %gather_fusion.1 = bf16[16,3,128,128]{3,2,1,0:T(8,128)(2,1)S(1)} fusion(bf16[128,3,128,128]{3,2,1,0:T(8,128)(2,1)} %all-gather.2.cloned.1.call-done, s32[1024]{0:T(1024)S(1)} %pad_clamp_fusion.1), kind=kCustom, calls=%fused_computation.1 | custom fusion | bytes 3145792 | tf_op jit(solution)/shard_map/gather | solution.py:25
  118.0 0.2 copy_select_fusion
  118.2 0.0 copy-start.3
  118.2 0.0 copy-start.1
  118.2 4.0 %convert_bitcast_fusion.2 = bf16[8,16,16,8,128]{4,3,2,1,0:T(8,128)(2,1)S(1)} fusion(bf16[8,128,2048]{2,1,0:T(8,128)(2,1)} %bitcast.73, bf16[16,3,128,128]{3,2,0,1:T(8,128)(2,1)S(1)} %copy_select_fusion, s32[]{:T(128)S(6)} %select_n.62), kind=kOutput, calls=%fused_computation.18 | convolution fusion | flops 538968064 | bytes 8650756 | tf_op jit(solution)/shard_map/iac,icx->iax/dot_general | solution.py:31
  122.3 0.0 copy-done.1
  122.3 1.2 convert_bitcast_fusion.1
  123.5 1.3 fusion.4
  124.9 1.2 convert_bitcast_fusion
  126.1 0.0 copy-done.3
  126.1 4.5 %fusion.1 = f32[16,128,8,128]{3,1,2,0:T(8,128)} fusion(bf16[8,16,16,8,128]{4,3,2,1,0:T(8,128)(2,1)S(1)} %convert_bitcast_fusion, bf16[16,3,128,128]{3,2,0,1:T(8,128)(2,1)S(1)} %copy_select_fusion), kind=kOutput, calls=%fused_computation.7 | convolution fusion | flops 536870912 | bytes 13107200 | tf_op jit(solution)/shard_map/iajd,jbd->iajb/dot_general | solution.py:35
  130.6 5.9 %fusion = bf16[8,128,16,128]{1,3,0,2:T(8,128)(2,1)} fusion(f32[16,128,8,128]{3,1,2,0:T(8,128)} %fusion.1, f32[16,128,8,128]{3,1,2,0:T(8,128)S(1)} %fusion.4, bf16[8,16,16,8,128]{4,3,2,1,0:T(8,128)(2,1)S(1)} %convert_bitcast_fusion.2, bf16[16,3,128,128]{3,2,0,1:T(8,128)(2,1)} %copy-done.3), kind=kOutput, calls=%fused_computation.5 | convolution fusion | flops 543162368 | bytes 25690112 | tf_op jit(solution)/shard_map/iajd,jbd->iajb/dot_general | solution.py:35
  136.5 6.8 %copy.20 = bf16[8,128,16,128]{3,2,1,0:T(8,128)(2,1)} copy(bf16[8,128,16,128]{1,3,0,2:T(8,128)(2,1)} %fusion) | data formatting | bytes 8388608 | tf_op jit(solution)/shard_map/convert_element_type | solution.py:40
  143.3 6.2 %copy.44 = bf16[128,8,16,128]{3,1,2,0:T(8,128)(2,1)} copy(bf16[128,8,16,128]{3,2,1,0:T(8,128)(2,1)} %bitcast.77) | data formatting | bytes 8388608
  149.6 0.0 reduce-scatter.2.cloned.1.call-update
  149.6 0.6 gather_fusion.2
  150.2 0.1 copy-done.4
  150.3 0.2 fusion.15
  150.5 0.0 copy-done.2
  150.5 0.6 gather_fusion.3
  151.1 0.6 fusion.19
  151.7 1.3 subtract_bitcast_fusion.1
  153.0 0.1 dynamic_slice.15
  153.1 50.4 %reduce-scatter.2.cloned.1.call-done = bf16[128,2048]{1,0:T(8,128)(2,1)} async-done(((bf16[1024,2048]{1,0:T(8,128)(2,1)}), bf16[128,2048]{1,0:T(8,128)(2,1)}) %reduce-scatter.2.cloned.1.call-update) | async-done | bytes 524304 | tf_op jit(solution)/shard_map/reduce_scatter | solution.py:39
  203.5 2.2 %add_divide_fusion = f32[128,2048]{1,0:T(8,128)} fusion(bf16[128,2048]{1,0:T(8,128)(2,1)} %reduce-scatter.2.cloned.1.call-done, f32[2048]{0:T(1024)S(1)} %get-tuple-element.6, f32[128]{0:T(128)S(1)} %dynamic_slice.15), kind=kLoop, calls=%fused_computation.20 | loop fusion | flops 786432 | bytes 1581568 | tf_op jit(solution)/shard_map/div | solution.py:50
  (10 shorter events, 0.1 us)
Async XLA Ops:
  6.5 143.1 %copy-start = (f32[128,128]{1,0:T(8,128)S(1)}, f32[128,128]{1,0:T(8,128)}, u32[]{:S(2)}) copy-start(f32[128,128]{1,0:T(8,128)} %param.13) | copy-start | bytes 196612
  6.5 106.1 %all-gather.2.cloned.1.call-start = ((), (), s32[]{:S(2)}) async-start(), calls=%async_computation.1 | async-start | bytes 12779520 | tf_op jit(solution)/shard_map/all_gather | solution.py:21
  7.3 196.3 %reduce-scatter.2.cloned.1.call-start = ((), (), s32[]{:S(2)}) async-start(), calls=%async_computation.2 | async-start | bytes 4718592 | tf_op jit(solution)/shard_map/reduce_scatter | solution.py:39
  118.2 7.9 %copy-start.3 = (bf16[16,3,128,128]{3,2,0,1:T(8,128)(2,1)}, bf16[16,3,128,128]{3,2,0,1:T(8,128)(2,1)S(1)}, u32[]{:S(2)}) copy-start(bf16[16,3,128,128]{3,2,0,1:T(8,128)(2,1)S(1)} %copy_select_fusion) | copy-start | bytes 4718596
  118.2 4.1 %copy-start.1 = (bf16[1024,2048]{1,0:T(8,128)(2,1)S(1)}, bf16[1024,2048]{1,0:T(8,128)(2,1)}, u32[]{:S(2)}) copy-start(bf16[1024,2048]{1,0:T(8,128)(2,1)} %param.7) | copy-start | bytes 12582916
  149.6 0.7 copy-start.4
  149.6 0.9 copy-start.2
Sparse Core Ops, SparseCore 0:
  10.7 101.8 all-gather.1
  149.7 53.7 reduce-scatter.1
where the time goes:
time: 213 us
  waiting for transfers between devices  154 us (72%)
  local copies, waits for them, and re-layouts  22.8 us (11%)
  matrix products  18.3 us (9%)
  between operations  13.6 us (6%)
  other arithmetic  3.71 us (2%)
    all_gather x1, waiting for transfers between devices, local(): segment = lax.all_gather(factors, 'pair', axis=0, tiled=True)  103 us
    reduce_scatter x1, waiting for transfers between devices, local(): lax.psum_scatter(partial_value.astype(jnp.bfloat16), 'cuts', scatter_dime...  50.4 us
    dot_general x3, matrix products, local(): jnp.einsum('iajd,jbd->iajb', half_done, picked[:, vector], preferred_elem...  11.7 us
    convert_element_type x1, local copies, waits for them, and re-layouts, local(): partial_value.astype(jnp.bfloat16)  6.81 us
    dot_general x3, matrix products, local(): jnp.einsum('iac,icx->iax', factor_left, blocks, preferred_element_type=jn...  6.52 us
    unnamed x11, local copies, waits for them, and re-layouts  6.33 us
    gather x1, local copies, waits for them, and re-layouts, local(): segment[safe_rows]  5.42 us
  transfers between devices with their start and end apart: 2, of which 2 were waited for; matrix products, arithmetic and copies ran while one was open for 3% of the time, Pallas kernels for 0%

commit v1 on v0

v1 whole, which is shorter than its diff:
```python
import jax
import jax.numpy as jnp
from jax import lax
from jax.experimental import pallas as pl
from jax.experimental.pallas import tpu as pltpu
from jax.sharding import PartitionSpec as P

TILE = 128
K = 16
NQ = 3
NZ, NX, NC, NY = 8, 4, 2, 8
NS = NX * NC
SL = TILE // NS
SLOTS = 128
BLOCK = SLOTS // NZ
ROWS = 8
SUBS = 4
SJ = K // SUBS
BF16 = jnp.bfloat16
F32 = jnp.float32
MESH = pl.DeviceIdType.MESH

GATHER_ORDER = sorted(
    [(q, t) for q in range(NQ) for t in range(1, 5)], key=lambda a: a[1] + 1.5 * a[0]
)


def ladder_kernel(
    amp, fac, screen, slot_of, orb, occ, virt, out,
    a_buf, gath0, gath1, gath2, sel, tiles, half, part, snd, rcv, rec,
    a_sem, loc_sem, sp_s, sp_r, ag_s, ag_r, dl_s, dl_r, ex_s, ex_r, rs_s, rs_r,
):
    gath = (gath0, gath1, gath2)
    pair = lax.axis_index("pair")
    y = lax.axis_index("cuts")
    s = lax.rem(pair, NS)
    z = pair // NS
    x = s // NC
    core = lax.rem(s, NC)
    p = pair // NC

    def wrap(value, n):
        return lax.rem(value + n, n)

    z_up, z_down = wrap(z + 1, NZ) * NS + s, wrap(z - 1, NZ) * NS + s
    y_up, y_down = wrap(y + 1, NY), wrap(y - 1, NY)

    load_a = pltpu.make_async_copy(amp, a_buf, a_sem)
    load_a.start()

    barrier = pltpu.get_barrier_semaphore()
    peers = [(z * NS + wrap(s + d, NS), y) for d in range(1, NS)]
    peers += [(z_up, y), (z_down, y), (pair, y_up), (pair, y_down)]
    for peer in peers:
        pl.semaphore_signal(barrier, inc=1, device_id=peer, device_id_type=MESH)
    pl.semaphore_wait(barrier, len(peers))

    def remote(src, dst, send, recv, device):
        copy = pltpu.make_async_remote_copy(
            src_ref=src, dst_ref=dst, send_sem=send, recv_sem=recv,
            device_id=device, device_id_type=MESH,
        )
        copy.start()
        return copy

    sent = []

    spread = {}
    mine = pl.ds(z * BLOCK + s * 2, 2)
    for q in range(NQ):
        rows = pl.ds(pl.multiple_of(s * SL, SL), SL)
        own = pltpu.make_async_copy(fac.at[:, q, rows, :], gath[q].at[mine], loc_sem.at[q])
        own.start()
        spread[q] = [own]
        for d in range(1, NS):
            to = wrap(s + d, NS)
            rows = pl.ds(pl.multiple_of(to * SL, SL), SL)
            spread[q].append(
                remote(
                    fac.at[:, q, rows, :], gath[q].at[mine],
                    sp_s.at[q, d - 1], sp_r.at[q, d - 1], (z * NS + to, y),
                )
            )
        sent += spread[q][1:]

    first = occ[orb[0, p]]
    second = occ[orb[1, p]]
    row = virt[pl.ds(screen[core * ROWS + y, p], 1), :] - first
    row = jnp.transpose(jnp.broadcast_to(row, (TILE, TILE)))

    def denominator(j, _):
        col = virt[pl.ds(screen[j, p], 1), :] - second
        rec[j] = 1.0 / (row + col)
        return 0

    lax.fori_loop(0, K, denominator, 0)

    ring = {}

    def gather_step(q, t):
        if t == 1:
            spread[q][0].wait()
            for copy in spread[q][1:]:
                copy.wait_recv()
        for way in range(2):
            if t > 1:
                ring[q, t - 1, way].wait_recv()
            if way == 0:
                start, to = wrap(z - (t - 1), NZ) * BLOCK, z_up
            else:
                start, to = wrap(z + (t - 1), NZ) * BLOCK, z_down
            count = BLOCK
            if t == NZ // 2:
                count = BLOCK // 2
                start = start + way * count
            block = gath[q].at[pl.ds(start, count)]
            ring[q, t, way] = remote(
                block, block, ag_s.at[q, t - 1, way], ag_r.at[q, t - 1, way], (to, y)
            )
            sent.append(ring[q, t, way])

    delivered = {}

    def deliver(q):
        for way in range(2):
            ring[q, NZ // 2, way].wait_recv()
        lanes = pl.ds(q * TILE, TILE)
        rows = pl.ds(pl.multiple_of(s * SL, SL), SL)
        for dx in (2, 1, 3, 0):
            to = wrap(x + dx, NX)
            its_pair = z * NX + to

            def pick(k, _):
                value = gath[q][slot_of[screen[k, its_pair]]]
                if dx == 0:
                    tiles[k, rows, lanes] = value
                else:
                    sel[q, dx - 1, k] = value
                return 0

            lax.fori_loop(0, K, pick, 0, unroll=4)
            if dx:
                delivered[q, dx] = remote(
                    sel.at[q, dx - 1], tiles.at[:, rows, lanes],
                    dl_s.at[q, dx - 1], dl_r.at[q, dx - 1], (z * NS + to * NC + core, y),
                )
                sent.append(delivered[q, dx])

    exchanged = {}

    def exchange(q):
        lanes = pl.ds(q * TILE, TILE)
        for dx in (0, 1, 3, 2):
            if dx:
                delivered[q, dx].wait_recv()
            rows = pl.ds(pl.multiple_of((wrap(x - dx, NX) * NC + core) * SL, SL), SL)
            block = tiles.at[:, rows, lanes]
            exchanged[q, dx] = remote(
                block, block, ex_s.at[q, dx], ex_r.at[q, dx], (z * NS + x * NC + 1 - core, y)
            )
            sent.append(exchanged[q, dx])

    def first_product(q):
        for dx in range(NX):
            exchanged[q, dx].wait_recv()
        lanes = pl.ds(q * TILE, TILE)

        def one_row(i, _):
            left = tiles[core * ROWS + i, :, lanes]
            rows = pl.ds(pl.multiple_of(i * TILE, TILE), TILE)
            for c in range(4):
                value = jnp.dot(
                    left, a_buf[rows, c * 512 : (c + 1) * 512], preferred_element_type=F32
                ).astype(BF16)
                for jj in range(4):
                    half[i, c * 4 + jj, :, lanes] = value[:, jj * TILE : (jj + 1) * TILE]
            return 0

        lax.fori_loop(0, ROWS, one_row, 0)

    for q, t in GATHER_ORDER:
        gather_step(q, t)
        if (q, t) == (1, 3):
            deliver(0)
        if (q, t) == (2, 2):
            exchange(0)
        if (q, t) == (2, 3):
            deliver(1)
    load_a.wait()
    first_product(0)
    exchange(1)
    deliver(2)
    first_product(1)
    exchange(2)
    first_product(2)

    def partial(r, slot):
        def one_column(j, _):
            part[slot, j] = lax.dot_general(
                half[r, j], tiles[j], (((1,), (1,)), ((), ())), preferred_element_type=F32
            )
            return 0

        lax.fori_loop(0, K, one_column, 0, unroll=2)

    moved = {}

    def send(way, t, sub, slot, add):
        value = part[slot, sub * SJ : (sub + 1) * SJ]
        if add:
            moved[way, t - 1, sub].wait_recv()
            value = value + rcv[way, t - 2, sub].astype(F32)
        snd[way, t - 1, sub] = value.astype(BF16)
        moved[way, t, sub] = remote(
            snd.at[way, t - 1, sub], rcv.at[way, t - 1, sub],
            rs_s.at[way, t - 1, sub], rs_r.at[way, t - 1, sub],
            (pair, y_up if way == 0 else y_down),
        )
        sent.append(moved[way, t, sub])

    long_subs = ((0, 1), (2, 3))
    short_subs = ((2, 3), (0, 1))
    partial(wrap(y + 4, NY), 0)
    for n in range(2):
        for way in range(2):
            send(way, 1, long_subs[way][n], 0, False)
    for t in range(2, 5):
        partial(wrap(y + 5 - t, NY), 0)
        partial(wrap(y - 5 + t, NY), 1)
        for n in range(2):
            for way in range(2):
                send(way, t, short_subs[way][n], way, t > 2)
        for n in range(2):
            for way in range(2):
                send(way, t, long_subs[way][n], way, True)
    partial(y, 0)
    for n in (2, 0, 3, 1):
        for way in range(2):
            moved[way, 4, n].wait_recv()
        for j in range(n * SJ, (n + 1) * SJ):
            value = part[0, j] + rcv[0, 3, n, j - n * SJ].astype(F32)
            value = value + rcv[1, 3, n, j - n * SJ].astype(F32)
            out[:, j * TILE : (j + 1) * TILE] = value * rec[j]
    for copy in sent:
        copy.wait_send()


def local(
    amplitudes, factors, screening, tile_slot, pair_orbitals, occupied_energy, virtual_energy
):
    anywhere = pl.BlockSpec(memory_space=pl.ANY)
    smem = pl.BlockSpec(memory_space=pltpu.SMEM)
    vmem = pl.BlockSpec(memory_space=pltpu.VMEM)
    dma = pltpu.SemaphoreType.DMA
    return pl.pallas_call(
        ladder_kernel,
        out_shape=jax.ShapeDtypeStruct((TILE, K * TILE), F32),
        in_specs=[anywhere, anywhere, smem, smem, smem, smem, vmem],
        out_specs=vmem,
        scratch_shapes=[
            pltpu.VMEM((ROWS * TILE, K * TILE), BF16),
            pltpu.VMEM((SLOTS, SL, TILE), BF16),
            pltpu.VMEM((SLOTS, SL, TILE), BF16),
            pltpu.VMEM((SLOTS, SL, TILE), BF16),
            pltpu.VMEM((NQ, NX - 1, K, SL, TILE), BF16),
            pltpu.VMEM((K, TILE, NQ * TILE), BF16),
            pltpu.VMEM((ROWS, K, TILE, NQ * TILE), BF16),
            pltpu.VMEM((2, K, TILE, TILE), F32),
            pltpu.VMEM((2, 4, SUBS, SJ, TILE, TILE), BF16),
            pltpu.VMEM((2, 4, SUBS, SJ, TILE, TILE), BF16),
            pltpu.VMEM((K, TILE, TILE), F32),
            dma,
            dma((NQ,)),
            dma((NQ, NS - 1)),
            dma((NQ, NS - 1)),
            dma((NQ, 4, 2)),
            dma((NQ, 4, 2)),
            dma((NQ, NX - 1)),
            dma((NQ, NX - 1)),
            dma((NQ, NX)),
            dma((NQ, NX)),
            dma((2, 4, SUBS)),
            dma((2, 4, SUBS)),
        ],
        compiler_params=pltpu.CompilerParams(
            collective_id=0, has_side_effects=True, vmem_limit_bytes=48 * 1024 * 1024
        ),
    )(
        amplitudes, factors, screening.T, tile_slot, pair_orbitals.T, occupied_energy, virtual_energy
    )


def solution(mesh):
    return jax.shard_map(
        local,
        mesh=mesh,
        in_specs=(P("pair", None), P("pair", "cuts", None, None), P(), P(), P(), P(), P()),
        out_specs=P(("pair", "cuts"), None),
        check_vma=False,
    )
```

time: 213 us -> 108 us (0.51)
  waiting for transfers between devices: 154 us -> 0 us
  Pallas kernels: 0 us -> 99.7 us
  matrix products: 18.3 us -> 0 us
  local copies, waits for them, and re-layouts: 22.8 us -> 7.67 us
  between operations: 13.6 us -> 0.02 us
  other arithmetic: 3.71 us -> 0 us
    all_gather x1 -> x0, waiting for transfers between devices: 103 us -> none  [local(): segment = lax.all_gather(factors, 'pair', axis=0, tiled=True)]
    pallas_call x0 -> x1, Pallas kernels: none -> 99.7 us  [local(): pl.pallas_call(ladder_kernel, out_shape=jax.ShapeDtypeStruct((TILE, K * T...]
    reduce_scatter x1 -> x0, waiting for transfers between devices: 50.4 us -> none  [local(): lax.psum_scatter(partial_value.astype(jnp.bfloat16), 'cuts', scatter_dime...]
    dot_general x6 -> x0, matrix products: 18.3 us -> none  [the longest x3 11.7 us: local(): jnp.einsum('iajd,jbd->iajb', half_done, picked[:, vector], preferred_elem...]
    gather x4 -> x0, local copies, waits for them, and re-layouts: 7.93 us -> none  [the longest x1 5.42 us: local(): segment[safe_rows]]
    convert_element_type x1 -> x0, local copies, waits for them, and re-layouts: 6.81 us -> none  [local(): partial_value.astype(jnp.bfloat16)]
    div x1 -> x0, other arithmetic: 2.22 us -> none  [local(): return summed / (row_part[:, None] + col_energy[None, :])]
    unnamed x11 -> x15, local copies, waits for them, and re-layouts: 6.33 us -> 7.67 us
  transfers between devices with their start and end apart: 2 -> 0, of which waited for: 2 -> 0; matrix products, arithmetic and copies ran while one was open for 3% -> 0% of each run, Pallas kernels for 0% -> 0%
where the time goes in v1:
time: 108 us; the launch traced here: 107 us
  Pallas kernels  99.7 us (92%)
  local copies, waits for them, and re-layouts  7.67 us (7%)
    pallas_call x1, Pallas kernels, local(): pl.pallas_call(ladder_kernel, out_shape=jax.ShapeDtypeStruct((TILE, K * T...  99.7 us
    unnamed x15, local copies, waits for them, and re-layouts  7.67 us

profile of v1, /device:TPU:1, one launch (start us, length us, event | category | flops | bytes accessed | tf_op | source)
XLA Modules:
  0.0 107.3 jit_solution(2256118681490083396)
XLA Ops:
  0.0 0.0 copy-start
  0.0 2.2 %copy-done = bf16[1024,2048]{1,0:T(8,128)(2,1)S(1)} copy-done((bf16[1024,2048]{1,0:T(8,128)(2,1)S(1)}, bf16[1024,2048]{1,0:T(8,128)(2,1)}, u32[]{:S(2)}) %copy-start) | copy-done | bytes 4194328
  2.2 0.0 copy-start.1
  2.2 0.9 copy-done.1
  3.1 0.0 copy-start.2
  3.1 0.8 copy-done.2
  4.0 0.0 copy-start.3
  4.0 0.7 copy-done.3
  4.7 0.0 copy-start.4
  4.7 0.7 copy-done.4
  5.4 0.0 copy-start.5
  5.4 0.7 copy-done.5
  6.1 0.0 copy-start.6
  6.1 0.7 copy-done.6
  6.7 99.7 %shard_map.73 = f32[128,2048]{1,0:T(8,128)S(1)} custom-call(bf16[1024,2048]{1,0:T(8,128)(2,1)S(1)} %copy-done, bf16[2,3,128,128]{3,2,1,0:T(8,128)(2,1)S(1)} %copy-done.1, s32[16,32]{1,0:T(8,128)S(1)} %bitcast.2, s32[128]{0:T(128)S(1)} %copy-done.6, s32[2,32]{1,0:T(2,128)S(1)} %bitcast.3, f32[4000]{0:T(1024)S(1)} %copy-done.3, f32[128,128]{1,0:T(8,128)S(1)} %copy-done.2), custom_call_target="tpu_custom_call" | custom-call | tf_op jit(solution)/shard_map/pallas_call | solution.py:255
  106.4 1.0 copy.9
Async XLA Ops:
  0.0 2.2 %copy-start = (bf16[1024,2048]{1,0:T(8,128)(2,1)S(1)}, bf16[1024,2048]{1,0:T(8,128)(2,1)}, u32[]{:S(2)}) copy-start(bf16[1024,2048]{1,0:T(8,128)(2,1)} %amp.1) | copy-start | bytes 12582916
  2.2 0.9 copy-start.1
  3.1 0.8 copy-start.2
  4.0 0.7 copy-start.3
  4.7 0.7 copy-start.4
  5.4 0.7 copy-start.5
  6.1 0.7 copy-start.6

commit v2 on v1

--- a/solution.py
+++ b/solution.py
@@ -12,6 +12,8 @@
 NS = NX * NC
 SL = TILE // NS
 SLOTS = 128
+PAIRS = 32
+NOCC = 4000
 BLOCK = SLOTS // NZ
 ROWS = 8
 SUBS = 4
@@ -21,14 +23,14 @@
 MESH = pl.DeviceIdType.MESH
 
 GATHER_ORDER = sorted(
-    [(q, t) for q in range(NQ) for t in range(1, 5)], key=lambda a: a[1] + 1.5 * a[0]
+    [(q, t) for q in range(NQ) for t in range(1, 5)], key=lambda a: a[1] + 0.1 * a[0]
 )
 
 
 def ladder_kernel(
-    amp, fac, screen, slot_of, orb, occ, virt, out,
+    amp, fac, screen_in, slot_in, orb_in, occ_in, virt_in, out,
     a_buf, gath0, gath1, gath2, sel, tiles, half, part, snd, rcv, rec,
-    a_sem, loc_sem, sp_s, sp_r, ag_s, ag_r, dl_s, dl_r, ex_s, ex_r, rs_s, rs_r,
+    screen, slot_of, orb, occ, virt, a_sem, in_sem, loc_sem, sp_s, sp_r, ag_s, ag_r, dl_s, dl_r, ex_s, ex_r, rs_s, rs_r,
 ):
     gath = (gath0, gath1, gath2)
     pair = lax.axis_index("pair")
@@ -47,6 +49,14 @@
 
     load_a = pltpu.make_async_copy(amp, a_buf, a_sem)
     load_a.start()
+    loads = [
+        pltpu.make_async_copy(src, dst, in_sem.at[n])
+        for n, (src, dst) in enumerate(
+            ((screen_in, screen), (slot_in, slot_of), (orb_in, orb), (occ_in, occ), (virt_in, virt))
+        )
+    ]
+    for load in loads:
+        load.start()
 
     barrier = pltpu.get_barrier_semaphore()
     peers = [(z * NS + wrap(s + d, NS), y) for d in range(1, NS)]
@@ -83,6 +93,8 @@
             )
         sent += spread[q][1:]
 
+    for load in loads:
+        load.wait()
     first = occ[orb[0, p]]
     second = occ[orb[1, p]]
     row = virt[pl.ds(screen[core * ROWS + y, p], 1), :] - first
@@ -180,19 +192,14 @@
 
     for q, t in GATHER_ORDER:
         gather_step(q, t)
-        if (q, t) == (1, 3):
-            deliver(0)
-        if (q, t) == (2, 2):
-            exchange(0)
-        if (q, t) == (2, 3):
-            deliver(1)
+    for q in range(NQ):
+        deliver(q)
     load_a.wait()
-    first_product(0)
-    exchange(1)
-    deliver(2)
-    first_product(1)
-    exchange(2)
-    first_product(2)
+    for q in range(NQ):
+        exchange(q)
+        if q:
+            first_product(q - 1)
+    first_product(NQ - 1)
 
     def partial(r, slot):
         def one_column(j, _):
@@ -248,14 +255,13 @@
 def local(
     amplitudes, factors, screening, tile_slot, pair_orbitals, occupied_energy, virtual_energy
 ):
-    anywhere = pl.BlockSpec(memory_space=pl.ANY)
-    smem = pl.BlockSpec(memory_space=pltpu.SMEM)
+    hbm = pl.BlockSpec(memory_space=pltpu.HBM)
     vmem = pl.BlockSpec(memory_space=pltpu.VMEM)
     dma = pltpu.SemaphoreType.DMA
     return pl.pallas_call(
         ladder_kernel,
         out_shape=jax.ShapeDtypeStruct((TILE, K * TILE), F32),
-        in_specs=[anywhere, anywhere, smem, smem, smem, smem, vmem],
+        in_specs=[hbm] * 7,
         out_specs=vmem,
         scratch_shapes=[
             pltpu.VMEM((ROWS * TILE, K * TILE), BF16),
@@ -269,7 +275,13 @@
             pltpu.VMEM((2, 4, SUBS, SJ, TILE, TILE), BF16),
             pltpu.VMEM((2, 4, SUBS, SJ, TILE, TILE), BF16),
             pltpu.VMEM((K, TILE, TILE), F32),
+            pltpu.SMEM((K, PAIRS), jnp.int32),
+            pltpu.SMEM((SLOTS,), jnp.int32),
+            pltpu.SMEM((2, PAIRS), jnp.int32),
+            pltpu.SMEM((NOCC,), F32),
+            pltpu.VMEM((SLOTS, TILE), F32),
             dma,
+            dma((5,)),
             dma((NQ,)),
             dma((NQ, NS - 1)),
             dma((NQ, NS - 1)),
@@ -283,7 +295,7 @@
             dma((2, 4, SUBS)),
         ],
         compiler_params=pltpu.CompilerParams(
-            collective_id=0, has_side_effects=True, vmem_limit_bytes=48 * 1024 * 1024
+            collective_id=0, has_side_effects=True, vmem_limit_bytes=60 * 1024 * 1024
         ),
     )(
         amplitudes, factors, screening.T, tile_slot, pair_orbitals.T, occupied_energy, virtual_energy

time: 108 us -> 97 us (0.90)
  local copies, waits for them, and re-layouts: 7.67 us -> 2.3 us
  Pallas kernels: 99.7 us -> 94.5 us
    unnamed x15 -> x1, local copies, waits for them, and re-layouts: 7.67 us -> 2.3 us
    pallas_call x1, Pallas kernels: 99.7 us -> 94.5 us  [local(): pl.pallas_call(ladder_kernel, out_shape=jax.ShapeDtypeStruct((TILE, K * T...]
where the time goes in v2:
time: 97 us; the launch traced here: 96.8 us
  Pallas kernels  94.5 us (97%)
  local copies, waits for them, and re-layouts  2.3 us (2%)
    pallas_call x1, Pallas kernels, local(): pl.pallas_call(ladder_kernel, out_shape=jax.ShapeDtypeStruct((TILE, K * T...  94.5 us
    unnamed x1, local copies, waits for them, and re-layouts  2.3 us

profile of v2, /device:TPU:1, one launch (start us, length us, event | category | flops | bytes accessed | tf_op | source)
XLA Modules:
  0.0 96.8 jit_solution(4082851896980324300)
XLA Ops:
  0.0 94.5 %shard_map.73 = f32[128,2048]{1,0:T(8,128)} custom-call(bf16[1024,2048]{1,0:T(8,128)(2,1)} %amp.1, bf16[2,3,128,128]{3,2,1,0:T(8,128)(2,1)} %fac.1, s32[16,32]{1,0:T(8,128)} %bitcast.2, s32[128]{0:T(128)} %slot_in.1, s32[2,32]{1,0:T(2,128)} %bitcast.3, f32[4000]{0:T(1024)} %occ_in.1, f32[128,128]{1,0:T(8,128)} %virt_in.1), custom_call_target="tpu_custom_call" | custom-call | tf_op jit(solution)/shard_map/pallas_call | solution.py:261
  94.5 2.3 %copy.9 = f32[128,2048]{1,0:T(8,128)} copy(f32[128,2048]{1,0:T(8,128)} %shard_map.73) | data formatting | bytes 2097152

commit v3 on v2

--- a/solution.py
+++ b/solution.py
@@ -18,19 +18,22 @@
 ROWS = 8
 SUBS = 4
 SJ = K // SUBS
+LEAD = NY // 2
 BF16 = jnp.bfloat16
 F32 = jnp.float32
 MESH = pl.DeviceIdType.MESH
 
-GATHER_ORDER = sorted(
-    [(q, t) for q in range(NQ) for t in range(1, 5)], key=lambda a: a[1] + 0.1 * a[0]
+SCHEDULE = (
+    ("g", 0, 1), ("g", 1, 1), ("g", 2, 1), ("g", 0, 2), ("g", 1, 2), ("g", 0, 3),
+    ("g", 2, 2), ("g", 0, 4), ("g", 1, 3), ("g", 2, 3), ("d", 0, 0), ("g", 1, 4),
+    ("g", 2, 4), ("d", 1, 0), ("e", 0, 0), ("d", 2, 0),
 )
 
 
 def ladder_kernel(
     amp, fac, screen_in, slot_in, orb_in, occ_in, virt_in, out,
     a_buf, gath0, gath1, gath2, sel, tiles, half, part, snd, rcv, rec,
-    screen, slot_of, orb, occ, virt, a_sem, in_sem, loc_sem, sp_s, sp_r, ag_s, ag_r, dl_s, dl_r, ex_s, ex_r, rs_s, rs_r,
+    screen, slot_of, wanted, orb, occ, virt, a_sem, in_sem, loc_sem, sp_s, sp_r, ag_s, ag_r, dl_s, dl_r, ex_s, ex_r, rs_s, rs_r,
 ):
     gath = (gath0, gath1, gath2)
     pair = lax.axis_index("pair")
@@ -95,6 +98,13 @@
 
     for load in loads:
         load.wait()
+    for dx in range(NX):
+
+        def want(k, _):
+            wanted[dx, k] = slot_of[screen[k, z * NX + wrap(x + dx, NX)]]
+            return 0
+
+        lax.fori_loop(0, K, want, 0)
     first = occ[orb[0, p]]
     second = occ[orb[1, p]]
     row = virt[pl.ds(screen[core * ROWS + y, p], 1), :] - first
@@ -140,17 +150,12 @@
         rows = pl.ds(pl.multiple_of(s * SL, SL), SL)
         for dx in (2, 1, 3, 0):
             to = wrap(x + dx, NX)
-            its_pair = z * NX + to
-
-            def pick(k, _):
-                value = gath[q][slot_of[screen[k, its_pair]]]
+            for k in range(K):
+                value = gath[q][wanted[dx, k]]
                 if dx == 0:
                     tiles[k, rows, lanes] = value
                 else:
                     sel[q, dx - 1, k] = value
-                return 0
-
-            lax.fori_loop(0, K, pick, 0, unroll=4)
             if dx:
                 delivered[q, dx] = remote(
                     sel.at[q, dx - 1], tiles.at[:, rows, lanes],
@@ -172,12 +177,14 @@
             )
             sent.append(exchanged[q, dx])
 
-    def first_product(q):
-        for dx in range(NX):
-            exchanged[q, dx].wait_recv()
+    def first_product(q, start=0, count=ROWS):
+        if start == 0:
+            for dx in range(NX):
+                exchanged[q, dx].wait_recv()
         lanes = pl.ds(q * TILE, TILE)
 
-        def one_row(i, _):
+        def one_row(n, _):
+            i = wrap(y + LEAD + n, ROWS)
             left = tiles[core * ROWS + i, :, lanes]
             rows = pl.ds(pl.multiple_of(i * TILE, TILE), TILE)
             for c in range(4):
@@ -188,27 +195,30 @@
                     half[i, c * 4 + jj, :, lanes] = value[:, jj * TILE : (jj + 1) * TILE]
             return 0
 
-        lax.fori_loop(0, ROWS, one_row, 0)
-
-    for q, t in GATHER_ORDER:
-        gather_step(q, t)
-    for q in range(NQ):
-        deliver(q)
+        lax.fori_loop(start, start + count, one_row, 0)
+
+    for step in SCHEDULE:
+        if step[0] == "g":
+            gather_step(step[1], step[2])
+        elif step[0] == "d":
+            deliver(step[1])
+        else:
+            exchange(step[1])
     load_a.wait()
-    for q in range(NQ):
-        exchange(q)
-        if q:
-            first_product(q - 1)
-    first_product(NQ - 1)
-
-    def partial(r, slot):
+    first_product(0)
+    exchange(1)
+    first_product(1)
+    exchange(2)
+    first_product(2, 0, 1)
+
+    def partial(r, slot, start=0, count=K):
         def one_column(j, _):
             part[slot, j] = lax.dot_general(
                 half[r, j], tiles[j], (((1,), (1,)), ((), ())), preferred_element_type=F32
             )
             return 0
 
-        lax.fori_loop(0, K, one_column, 0, unroll=2)
+        lax.fori_loop(start, start + count, one_column, 0, unroll=2)
 
     moved = {}
 
@@ -227,10 +237,12 @@
 
     long_subs = ((0, 1), (2, 3))
     short_subs = ((2, 3), (0, 1))
-    partial(wrap(y + 4, NY), 0)
     for n in range(2):
         for way in range(2):
-            send(way, 1, long_subs[way][n], 0, False)
+            sub = long_subs[way][n]
+            partial(wrap(y + LEAD, NY), 0, sub * SJ, SJ)
+            send(way, 1, sub, 0, False)
+    first_product(2, 1, ROWS - 1)
     for t in range(2, 5):
         partial(wrap(y + 5 - t, NY), 0)
         partial(wrap(y - 5 + t, NY), 1)
@@ -277,6 +289,7 @@
             pltpu.VMEM((K, TILE, TILE), F32),
             pltpu.SMEM((K, PAIRS), jnp.int32),
             pltpu.SMEM((SLOTS,), jnp.int32),
+            pltpu.SMEM((NX, K), jnp.int32),
             pltpu.SMEM((2, PAIRS), jnp.int32),
             pltpu.SMEM((NOCC,), F32),
             pltpu.VMEM((SLOTS, TILE), F32),

time: 97 us -> 96.4 us (level)
  no operation moved by 1% of the time
where the time goes in v3:
time: 96.4 us; the launch traced here: 96.3 us
  Pallas kernels  94 us (98%)
  local copies, waits for them, and re-layouts  2.3 us (2%)
    pallas_call x1, Pallas kernels, local(): pl.pallas_call(ladder_kernel, out_shape=jax.ShapeDtypeStruct((TILE, K * T...  94 us
    unnamed x1, local copies, waits for them, and re-layouts  2.3 us

profile of v3, /device:TPU:1, one launch (start us, length us, event | category | flops | bytes accessed | tf_op | source)
XLA Modules:
  0.0 96.3 jit_solution(10658862984633649771)
XLA Ops:
  0.0 94.0 %shard_map.73 = f32[128,2048]{1,0:T(8,128)} custom-call(bf16[1024,2048]{1,0:T(8,128)(2,1)} %amp.1, bf16[2,3,128,128]{3,2,1,0:T(8,128)(2,1)} %fac.1, s32[16,32]{1,0:T(8,128)} %bitcast.2, s32[128]{0:T(128)} %slot_in.1, s32[2,32]{1,0:T(2,128)} %bitcast.3, f32[4000]{0:T(1024)} %occ_in.1, f32[128,128]{1,0:T(8,128)} %virt_in.1), custom_call_target="tpu_custom_call" | custom-call | tf_op jit(solution)/shard_map/pallas_call | solution.py:273
  94.0 2.3 %copy.9 = f32[128,2048]{1,0:T(8,128)} copy(f32[128,2048]{1,0:T(8,128)} %shard_map.73) | data formatting | bytes 2097152

commit v4 on v3

--- a/solution.py
+++ b/solution.py
@@ -267,14 +267,16 @@
 def local(
     amplitudes, factors, screening, tile_slot, pair_orbitals, occupied_energy, virtual_energy
 ):
+    arrays = (
+        amplitudes, factors, screening.T, tile_slot, pair_orbitals.T, occupied_energy, virtual_energy
+    )
     hbm = pl.BlockSpec(memory_space=pltpu.HBM)
-    vmem = pl.BlockSpec(memory_space=pltpu.VMEM)
     dma = pltpu.SemaphoreType.DMA
     return pl.pallas_call(
         ladder_kernel,
         out_shape=jax.ShapeDtypeStruct((TILE, K * TILE), F32),
         in_specs=[hbm] * 7,
-        out_specs=vmem,
+        out_specs=pl.BlockSpec(memory_space=pltpu.VMEM),
         scratch_shapes=[
             pltpu.VMEM((ROWS * TILE, K * TILE), BF16),
             pltpu.VMEM((SLOTS, SL, TILE), BF16),
@@ -308,11 +310,9 @@
             dma((2, 4, SUBS)),
         ],
         compiler_params=pltpu.CompilerParams(
-            collective_id=0, has_side_effects=True, vmem_limit_bytes=60 * 1024 * 1024
+            collective_id=0, has_side_effects=True, vmem_limit_bytes=48 * 1024 * 1024
         ),
-    )(
-        amplitudes, factors, screening.T, tile_slot, pair_orbitals.T, occupied_energy, virtual_energy
-    )
+    )(*(pltpu.with_memory_space_constraint(array, pltpu.HBM) for array in arrays))
 
 
 def solution(mesh):

time: 96.4 us -> 94.1 us (0.976)
  local copies, waits for them, and re-layouts: 2.3 us -> 0.97 us
  Pallas kernels: 94 us -> 93 us
    unnamed x1, local copies, waits for them, and re-layouts: 2.3 us -> 0.97 us
    pallas_call x1, Pallas kernels: 94 us -> 93 us  [local(): pl.pallas_call(ladder_kernel, out_shape=jax.ShapeDtypeStruct((TILE, K * T...]
where the time goes in v4:
time: 94.1 us; the launch traced here: 94 us
  Pallas kernels  93 us (99%)
  local copies, waits for them, and re-layouts  0.97 us (1%)
    pallas_call x1, Pallas kernels, local(): pl.pallas_call(ladder_kernel, out_shape=jax.ShapeDtypeStruct((TILE, K * T...  93 us

profile of v4, /device:TPU:1, one launch (start us, length us, event | category | flops | bytes accessed | tf_op | source)
XLA Modules:
  0.0 94.0 jit_solution(5306337974339355249)
XLA Ops:
  0.0 93.0 %shard_map.73 = f32[128,2048]{1,0:T(8,128)S(1)} custom-call(bf16[1024,2048]{1,0:T(8,128)(2,1)} %amp.1, bf16[2,3,128,128]{3,2,1,0:T(8,128)(2,1)} %fac.1, s32[16,32]{1,0:T(8,128)} %bitcast.2, s32[128]{0:T(128)} %slot_in.1, s32[2,32]{1,0:T(2,128)} %bitcast.3, f32[4000]{0:T(1024)} %occ_in.1, f32[128,128]{1,0:T(8,128)} %virt_in.1), custom_call_target="tpu_custom_call" | custom-call | tf_op jit(solution)/shard_map/pallas_call | solution.py:275
  93.0 1.0 %copy.9 = f32[128,2048]{1,0:T(8,128)} copy(f32[128,2048]{1,0:T(8,128)S(1)} %shard_map.73) | data formatting | bytes 2097152

commit v5 on v4

--- a/solution.py
+++ b/solution.py
@@ -85,7 +85,7 @@
         own = pltpu.make_async_copy(fac.at[:, q, rows, :], gath[q].at[mine], loc_sem.at[q])
         own.start()
         spread[q] = [own]
-        for d in range(1, NS):
+        for d in (4, 3, 5, 2, 6, 1, 7):
             to = wrap(s + d, NS)
             rows = pl.ds(pl.multiple_of(to * SL, SL), SL)
             spread[q].append(
@@ -96,26 +96,30 @@
             )
         sent += spread[q][1:]
 
-    for load in loads:
-        load.wait()
-    for dx in range(NX):
-
-        def want(k, _):
-            wanted[dx, k] = slot_of[screen[k, z * NX + wrap(x + dx, NX)]]
+    def look_up():
+        for load in loads:
+            load.wait()
+        for dx in range(NX):
+            its_pair = z * NX + wrap(x + dx, NX)
+
+            def want(k, _):
+                wanted[dx, k] = slot_of[screen[k, its_pair]]
+                return 0
+
+            lax.fori_loop(0, K, want, 0, unroll=4)
+
+    def denominators():
+        first = occ[orb[0, p]]
+        second = occ[orb[1, p]]
+        row = virt[pl.ds(screen[core * ROWS + y, p], 1), :] - first
+        row = jnp.transpose(jnp.broadcast_to(row, (TILE, TILE)))
+
+        def denominator(j, _):
+            col = virt[pl.ds(screen[j, p], 1), :] - second
+            rec[j] = 1.0 / (row + col)
             return 0
 
-        lax.fori_loop(0, K, want, 0)
-    first = occ[orb[0, p]]
-    second = occ[orb[1, p]]
-    row = virt[pl.ds(screen[core * ROWS + y, p], 1), :] - first
-    row = jnp.transpose(jnp.broadcast_to(row, (TILE, TILE)))
-
-    def denominator(j, _):
-        col = virt[pl.ds(screen[j, p], 1), :] - second
-        rec[j] = 1.0 / (row + col)
-        return 0
-
-    lax.fori_loop(0, K, denominator, 0)
+        lax.fori_loop(0, K, denominator, 0)
 
     ring = {}
 
@@ -204,11 +208,13 @@
             deliver(step[1])
         else:
             exchange(step[1])
+        if step == ("g", 2, 1):
+            look_up()
     load_a.wait()
+    exchange(1)
     first_product(0)
-    exchange(1)
+    exchange(2)
     first_product(1)
-    exchange(2)
     first_product(2, 0, 1)
 
     def partial(r, slot, start=0, count=K):
@@ -243,6 +249,7 @@
             partial(wrap(y + LEAD, NY), 0, sub * SJ, SJ)
             send(way, 1, sub, 0, False)
     first_product(2, 1, ROWS - 1)
+    denominators()
     for t in range(2, 5):
         partial(wrap(y + 5 - t, NY), 0)
         partial(wrap(y - 5 + t, NY), 1)

time: 94.1 us -> 91.6 us (0.973)
  Pallas kernels: 93 us -> 90.5 us
    pallas_call x1, Pallas kernels: 93 us -> 90.5 us  [local(): pl.pallas_call(ladder_kernel, out_shape=jax.ShapeDtypeStruct((TILE, K * T...]
where the time goes in v5:
time: 91.6 us; the launch traced here: 91.5 us
  Pallas kernels  90.5 us (99%)
  local copies, waits for them, and re-layouts  0.97 us (1%)
    pallas_call x1, Pallas kernels, local(): pl.pallas_call(ladder_kernel, out_shape=jax.ShapeDtypeStruct((TILE, K * T...  90.5 us

profile of v5, /device:TPU:1, one launch (start us, length us, event | category | flops | bytes accessed | tf_op | source)
XLA Modules:
  0.0 91.5 jit_solution(7024297720721506686)
XLA Ops:
  0.0 90.5 %shard_map.73 = f32[128,2048]{1,0:T(8,128)S(1)} custom-call(bf16[1024,2048]{1,0:T(8,128)(2,1)} %amp.1, bf16[2,3,128,128]{3,2,1,0:T(8,128)(2,1)} %fac.1, s32[16,32]{1,0:T(8,128)} %bitcast.2, s32[128]{0:T(128)} %slot_in.1, s32[2,32]{1,0:T(2,128)} %bitcast.3, f32[4000]{0:T(1024)} %occ_in.1, f32[128,128]{1,0:T(8,128)} %virt_in.1), custom_call_target="tpu_custom_call" | custom-call | tf_op jit(solution)/shard_map/pallas_call | solution.py:282
  90.5 1.0 %copy.9 = f32[128,2048]{1,0:T(8,128)} copy(f32[128,2048]{1,0:T(8,128)S(1)} %shard_map.73) | data formatting | bytes 2097152

commit v6 on v5

--- a/solution.py
+++ b/solution.py
@@ -224,7 +224,7 @@
             )
             return 0
 
-        lax.fori_loop(start, start + count, one_column, 0, unroll=2)
+        lax.fori_loop(start, start + count, one_column, 0, unroll=4)
 
     moved = {}
 

time: 91.6 us -> 89.7 us (0.979)
  Pallas kernels: 90.5 us -> 88.5 us
    pallas_call x1, Pallas kernels: 90.5 us -> 88.5 us  [local(): pl.pallas_call(ladder_kernel, out_shape=jax.ShapeDtypeStruct((TILE, K * T...]
where the time goes in v6:
time: 89.7 us; the launch traced here: 89.5 us
  Pallas kernels  88.5 us (99%)
  local copies, waits for them, and re-layouts  0.97 us (1%)
    pallas_call x1, Pallas kernels, local(): pl.pallas_call(ladder_kernel, out_shape=jax.ShapeDtypeStruct((TILE, K * T...  88.5 us

profile of v6, /device:TPU:1, one launch (start us, length us, event | category | flops | bytes accessed | tf_op | source)
XLA Modules:
  0.0 89.5 jit_solution(8641905039360226438)
XLA Ops:
  0.0 88.5 %shard_map.73 = f32[128,2048]{1,0:T(8,128)S(1)} custom-call(bf16[1024,2048]{1,0:T(8,128)(2,1)} %amp.1, bf16[2,3,128,128]{3,2,1,0:T(8,128)(2,1)} %fac.1, s32[16,32]{1,0:T(8,128)} %bitcast.2, s32[128]{0:T(128)} %slot_in.1, s32[2,32]{1,0:T(2,128)} %bitcast.3, f32[4000]{0:T(1024)} %occ_in.1, f32[128,128]{1,0:T(8,128)} %virt_in.1), custom_call_target="tpu_custom_call" | custom-call | tf_op jit(solution)/shard_map/pallas_call | solution.py:282
  88.5 1.0 %copy.9 = f32[128,2048]{1,0:T(8,128)} copy(f32[128,2048]{1,0:T(8,128)S(1)} %shard_map.73) | data formatting | bytes 2097152

commit v7 on v6

--- a/solution.py
+++ b/solution.py
@@ -224,7 +224,7 @@
             )
             return 0
 
-        lax.fori_loop(start, start + count, one_column, 0, unroll=4)
+        lax.fori_loop(start, start + count, one_column, 0, unroll=min(count, 8))
 
     moved = {}
 

time: 89.7 us -> 89.8 us (level)
  no operation moved by 1% of the time
where the time goes in v7:
time: 89.8 us; the launch traced here: 89.6 us
  Pallas kernels  88.7 us (99%)
  local copies, waits for them, and re-layouts  0.97 us (1%)
    pallas_call x1, Pallas kernels, local(): pl.pallas_call(ladder_kernel, out_shape=jax.ShapeDtypeStruct((TILE, K * T...  88.7 us

profile of v7, /device:TPU:1, one launch (start us, length us, event | category | flops | bytes accessed | tf_op | source)
XLA Modules:
  0.0 89.6 jit_solution(13160176311938848577)
XLA Ops:
  0.0 88.7 %shard_map.73 = f32[128,2048]{1,0:T(8,128)S(1)} custom-call(bf16[1024,2048]{1,0:T(8,128)(2,1)} %amp.1, bf16[2,3,128,128]{3,2,1,0:T(8,128)(2,1)} %fac.1, s32[16,32]{1,0:T(8,128)} %bitcast.2, s32[128]{0:T(128)} %slot_in.1, s32[2,32]{1,0:T(2,128)} %bitcast.3, f32[4000]{0:T(1024)} %occ_in.1, f32[128,128]{1,0:T(8,128)} %virt_in.1), custom_call_target="tpu_custom_call" | custom-call | tf_op jit(solution)/shard_map/pallas_call | solution.py:282
  88.7 1.0 %copy.9 = f32[128,2048]{1,0:T(8,128)} copy(f32[128,2048]{1,0:T(8,128)S(1)} %shard_map.73) | data formatting | bytes 2097152
